TPU v7x, 32 devices: a whole 2x2x4 slice. The times are simulated.
32 devices in a mesh: groups: 1, row: 16 (over z, y, core), col: 2 (over x).
Axes of the slice: x: 2, y: 2, z: 4, core: 2. Of those that a mesh axis runs over, the one named last changes fastest.
Arguments:
- pair_grid: bfloat16 [256, 256, 128], P(('groups', 'row'), 'col'), may hold values from -6 to 6
- alignment_pool: bfloat16 [256, 256, 64], P('groups', 'row'), may hold values from -6 to 6
- sample_index: int32 [64], P('groups'), may hold values from 0 to 255
- token_mask: int32 [256], P('groups'), may hold values 0 or 1
- outer_proj: bfloat16 [64, 64], replicated, may hold values from -0.75 to 0.75
- outer_mix: bfloat16 [1024, 128], replicated, may hold values from -0.375 to 0.375
- pair_logit: bfloat16 [128, 8], replicated, may hold values from -1 to 1
- average_proj: bfloat16 [64, 512], replicated, may hold values from -0.75 to 0.75
- average_mix: bfloat16 [256, 64], replicated, may hold values from -0.75 to 0.75
- triangle_proj: bfloat16 [128, 640], replicated, may hold values from -0.5 to 0.5
- triangle_mix: bfloat16 [128, 128], replicated, may hold values from -0.5 to 0.5
- transition_up: bfloat16 [128, 1024], replicated, may hold values from -0.5 to 0.5
- transition_down: bfloat16 [512, 128], replicated, may hold values from -0.25 to 0.25
Outputs:
- pair_next: bfloat16 [256, 256, 128], P(('groups', 'row'), 'col')
- alignment_next: bfloat16 [64, 256, 64], P('groups', 'row')
Inputs may be any that keep to these rules, and one draw needn't show every extreme that they name: `sample_index`: indices into the first dimension of alignment_pool; they may repeat. `token_mask`: 1 marks a real residue, 0 a padded one.
All inputs are finite; a program needn't handle non-finite values.
Results may differ from a plain program's by a relative error of at most 0.008.
Values may be sent and summed in bfloat16 or wider, within the bound.
A program may use at most 64 MiB of HBM per device.

v0:
```python
import jax
import jax.numpy as jnp
from jax import lax
from jax.sharding import PartitionSpec as P

epsilon = 1e-05


def normalize(values, channel_dim):
    values = values.astype(jnp.float32)
    centred = values - jnp.mean(values, axis=channel_dim, keepdims=True)
    spread = jnp.mean(centred * centred, axis=channel_dim, keepdims=True)
    return centred / jnp.sqrt(spread + epsilon)


def triangle_product(exchanged, n_row, n_col):
    left_part = exchanged[0]
    right_part = exchanged[1]
    item_count = left_part.shape[2]
    tok_row = left_part.shape[3]
    tok_col = left_part.shape[4]
    product = jnp.einsum(
        "ruxiq,suxjq->xrisj", left_part, right_part, preferred_element_type=jnp.float32
    )
    product = product.reshape(item_count, n_row, tok_row, n_col, tok_col)
    return product.transpose(1, 3, 0, 2, 4).astype(jnp.bfloat16)


def on_device(
    pair_grid,
    alignment_pool,
    sample_index,
    token_mask,
    outer_proj,
    outer_mix,
    pair_logit,
    average_proj,
    average_mix,
    triangle_proj,
    triangle_mix,
    transition_up,
    transition_down,
):
    n_row = lax.axis_size("row")
    n_col = lax.axis_size("col")
    tok_row = pair_grid.shape[0]
    tok_col = pair_grid.shape[1]
    pair_width = pair_grid.shape[2]
    samples = sample_index.shape[0]
    align_width = alignment_pool.shape[2]
    outer_width = outer_proj.shape[1] // 2
    head_count = pair_logit.shape[1]
    head_total = average_proj.shape[1] // 2
    head_dim = head_total // head_count
    inner_width = transition_down.shape[0]
    row_start = lax.axis_index("row") * tok_row
    column_start = lax.axis_index("col") * tok_col
    alignments = jnp.take(alignment_pool, sample_index, axis=0)
    align_norm = normalize(alignments, 2).astype(jnp.bfloat16)
    align_rows = align_norm.reshape(samples, tok_row * align_width)
    gathered = lax.all_gather(align_rows, "row", axis=1, tiled=True)
    column_flat = lax.dynamic_slice_in_dim(
        gathered, column_start * align_width, tok_col * align_width, 1
    )
    column_norm = column_flat.reshape(samples, tok_col, align_width)
    row_factor = jnp.dot(
        align_norm, outer_proj[:, :outer_width], preferred_element_type=jnp.float32
    ).astype(jnp.bfloat16)
    column_factor = jnp.dot(
        column_norm, outer_proj[:, outer_width:], preferred_element_type=jnp.float32
    ).astype(jnp.bfloat16)
    column_rows = column_factor.reshape(samples, tok_col * outer_width)
    block_rows = 8
    block_count = tok_row // block_rows
    row_blocks = row_factor.reshape(samples, block_count, block_rows * outer_width).transpose(
        1, 0, 2
    )
    pair_blocks = pair_grid.reshape(block_count, block_rows, tok_col, pair_width)

    def outer_step(operands):
        left_block, pair_block = operands
        outer_sum = lax.dot_general(
            left_block, column_rows, (((0,), (0,)), ((), ())), preferred_element_type=jnp.float32
        )
        outer_sum = outer_sum.reshape(block_rows, outer_width, tok_col, outer_width).transpose(
            0, 2, 1, 3
        )
        outer_mean = (
            (outer_sum * (1.0 / samples))
            .astype(jnp.bfloat16)
            .reshape(block_rows * tok_col, outer_width * outer_width)
        )
        update = jnp.dot(outer_mean, outer_mix, preferred_element_type=jnp.float32).reshape(
            block_rows, tok_col, pair_width
        )
        return (pair_block.astype(jnp.float32) + update).astype(jnp.bfloat16)

    pair_one = lax.map(outer_step, (row_blocks, pair_blocks)).reshape(tok_row, tok_col, pair_width)
    pair_norm = normalize(pair_one, 2).astype(jnp.bfloat16)
    value_weight = average_proj[:, :head_total].reshape(align_width, head_count, head_dim)
    gate_weight = average_proj[:, head_total:].reshape(align_width, head_count, head_dim)
    mix_weight = average_mix.reshape(head_count, head_dim, align_width)
    scores = lax.dot_general(
        pair_logit, pair_norm, (((0,), (2,)), ((), ())), preferred_element_type=jnp.float32
    )
    weights = jnp.exp(scores)
    partial_total = jnp.sum(weights, axis=2)
    weights_low = weights.astype(jnp.bfloat16)
    column_values = jnp.einsum(
        "sjm,mhc->hjsc", column_norm, value_weight, preferred_element_type=jnp.float32
    )
    column_values = column_values.astype(jnp.bfloat16).reshape(
        head_count, tok_col, samples * head_dim
    )
    partial_sum = jnp.einsum(
        "hij,hjk->hik", weights_low, column_values, preferred_element_type=jnp.float32
    )
    weighted, totals = (
        lax.psum(partial_sum.astype(jnp.bfloat16), "col").astype(jnp.float32),
        lax.psum(partial_total.astype(jnp.bfloat16), "col").astype(jnp.float32),
    )
    gate_values = jax.nn.sigmoid(
        jnp.einsum("sim,mhc->hisc", align_norm, gate_weight, preferred_element_type=jnp.float32)
    )
    weighted = weighted.reshape(head_count, tok_row, samples, head_dim)
    averaged = (gate_values * weighted / totals[:, :, None, None]).astype(jnp.bfloat16)
    align_update = jnp.einsum(
        "hisc,hcm->sim", averaged, mix_weight, preferred_element_type=jnp.float32
    )
    alignment_next = (alignments.astype(jnp.float32) + align_update).astype(jnp.bfloat16)
    flat_norm = pair_norm.reshape(tok_row * tok_col, pair_width)
    projected = lax.dot_general(
        triangle_proj[:, : 4 * pair_width],
        flat_norm,
        (((0,), (1,)), ((), ())),
        preferred_element_type=jnp.float32,
    )
    projected = projected.reshape(4, pair_width, tok_row, tok_col)
    row_mask = lax.dynamic_slice_in_dim(token_mask, row_start, tok_row, 0).astype(jnp.float32)
    column_mask = lax.dynamic_slice_in_dim(token_mask, column_start, tok_col, 0).astype(jnp.float32)
    pair_mask = row_mask[:, None] * column_mask[None, :]
    left_side = jax.nn.sigmoid(projected[0]) * projected[1] * pair_mask
    right_side = jax.nn.sigmoid(projected[2]) * projected[3] * pair_mask
    factors = jnp.stack([left_side, right_side]).astype(jnp.bfloat16)
    group_size = pair_width // (n_row * n_col)
    grouped = factors.reshape(2, n_row * n_col, group_size, tok_row, tok_col)
    received = lax.all_to_all(grouped, ("row", "col"), split_axis=1, concat_axis=1, tiled=True)
    arranged = received.reshape(2, n_row, n_col, received.shape[2], tok_row, tok_col)
    result = triangle_product(arranged, n_row, n_col)
    flat_result = result.reshape(n_row * n_col, result.shape[2], tok_row, tok_col)
    product = lax.all_to_all(flat_result, ("row", "col"), split_axis=0, concat_axis=0, tiled=True)
    product = product.reshape(pair_width, tok_row, tok_col)
    product_norm = normalize(product, 0).astype(jnp.bfloat16).reshape(pair_width, tok_row * tok_col)
    mixed = lax.dot_general(
        product_norm, triangle_mix, (((0,), (0,)), ((), ())), preferred_element_type=jnp.float32
    )
    gate_out = jax.nn.sigmoid(
        jnp.dot(flat_norm, triangle_proj[:, 4 * pair_width :], preferred_element_type=jnp.float32)
    )
    pair_two = (
        pair_one.reshape(tok_row * tok_col, pair_width).astype(jnp.float32) + gate_out * mixed
    ).astype(jnp.bfloat16)
    tail_rows = pair_two.reshape(block_count, block_rows * tok_col, pair_width)

    def transition_step(rows_block):
        normed = normalize(rows_block, 1).astype(jnp.bfloat16)
        expanded = jnp.dot(normed, transition_up, preferred_element_type=jnp.float32)
        hidden = (jax.nn.silu(expanded[:, :inner_width]) * expanded[:, inner_width:]).astype(
            jnp.bfloat16
        )
        return (
            rows_block.astype(jnp.float32)
            + jnp.dot(hidden, transition_down, preferred_element_type=jnp.float32)
        ).astype(jnp.bfloat16)

    pair_next = lax.map(transition_step, tail_rows).reshape(tok_row, tok_col, pair_width)
    return (pair_next, alignment_next)


def solution(mesh):
    in_specs = (
        P(("groups", "row"), "col", None),
        P("groups", "row", None),
        P("groups"),
        P("groups"),
        P(),
        P(),
        P(),
        P(),
        P(),
        P(),
        P(),
        P(),
        P(),
    )
    out_specs = (P(("groups", "row"), "col", None), P("groups", "row", None))
    return jax.shard_map(
        on_device, mesh=mesh, in_specs=in_specs, out_specs=out_specs, check_vma=False
    )
```

profile of v0, /device:TPU:0, one launch (start us, length us, event | category | flops | bytes accessed | tf_op | source)
XLA Modules:
  0.0 163.6 jit_solution(2614358065298384016)
XLA Ops:
  8.5 2.0 %copy.82 = bf16[256,16,64]{2,1,0:T(8,128)(2,1)S(1)} copy(bf16[256,16,64]{0,2,1:T(8,128)(2,1)} %param.18) | data formatting | bytes 1048576 | tf_op args[1]
  14.1 1.2 convolution_convert_fusion.2
  15.3 42.9 %all-gather.2.cloned.1.call-done = bf16[64,16384]{1,0:T(8,128)(2,1)} async-done(((bf16[64,1024]{1,0:T(8,128)(2,1)}), bf16[64,16384]{1,0:T(8,128)(2,1)}) %all-gather.2.cloned.1.call-update) | async-done | bytes 2097168 | tf_op jit(solution)/shard_map/all_gather | solution.py:61
  58.2 2.3 %constant_dynamic-slice_fusion.1 = bf16[64,8192]{1,0:T(8,128)(2,1)} fusion(bf16[64,16384]{1,0:T(8,128)(2,1)} %all-gather.2.cloned.1.call-done, s32[]{:T(128)S(6)} %select_n.24), kind=kLoop, calls=%fused_computation.116 | loop fusion | bytes 2097156 | tf_op jit(solution)/shard_map/dynamic_slice | solution.py:62
  60.5 3.3 %reshape.294 = bf16[64,128,64]{2,1,0:T(8,128)(2,1)S(1)} reshape(bf16[64,8192]{1,0:T(8,128)(2,1)} %constant_dynamic-slice_fusion.1) | data formatting | bytes 2097152 | tf_op jit(solution)/shard_map/reshape | solution.py:65
  63.8 1.3 copy-done.1
  65.1 0.9 convolution_convert_fusion.1
  66.0 1.7 %copy.89 = bf16[64,128,32]{0,2,1:T(8,128)(2,1)S(1)} copy(bf16[64,128,32]{1,2,0:T(8,128)(2,1)S(1)} %convolution_convert_fusion.1) | data formatting | bytes 1048576 | tf_op jit(solution)/shard_map/convert_element_type | solution.py:71
  67.7 9.3 %while.20 = (s32[]{:T(128)}, bf16[2,8,128,128]{3,2,1,0:T(8,128)(2,1)S(1)}, bf16[2,8,128,128]{3,2,1,0:T(8,128)(2,1)}, bf16[2,64,256]{1,2,0:T(8,128)(2,1)}, bf16[6...) while((s32[]{:T(128)}, bf16[2,8,128,128]{3,2,1,0:T(8,128)(2,1)S(1)}, ...), condition=%wide.region_3.4_spmd, body=%wide.region_2.3_spmd.sunk | while | flops 405143552 | bytes 13992077 | solution.py:98
  68.6 1.1 copy.148
  73.2 1.1 copy.148
  80.0 1.6 slice_multiply_fusion.2
  82.1 1.6 copy.91
  84.2 1.2 copy.92
  85.5 3.5 %all-to-all-start = ((bf16[2,32,4,16,128]{4,3,2,0,1:T(8,128)(2,1)}), bf16[2,32,4,16,128]{4,3,2,0,1:T(8,128)(2,1)}, u32[]{:S(2)}, u32[]{:S(2)}) async-start(bf16[2,32,4,16,128]{4,3,2,0,1:T(8,128)(2,1)} %copy.92), calls=%async_computation | async-start | bytes 2097152 | tf_op jit(solution)/shard_map/all_to_all | solution.py:147
  89.4 1.3 convert_bitcast_fusion.1
  92.5 1.2 convolution_convert_fusion
  93.7 1.6 %reshape.302 = bf16[8,16,64,32]{3,2,1,0:T(8,128)(2,1)S(1)} reshape(bf16[8,16,2048]{2,1,0:T(8,128)(2,1)S(1)} %convolution_convert_fusion) | data formatting | bytes 1048576 | tf_op jit(solution)/shard_map/reshape | solution.py:125
  95.3 1.6 copy.103
  97.0 18.1 %all-to-all-done = bf16[2,32,4,16,128]{4,3,2,0,1:T(8,128)(2,1)} async-done(((bf16[2,32,4,16,128]{4,3,2,0,1:T(8,128)(2,1)}), bf16[2,32,4,16,128]{4,3,2,0,1:T(8,128)(2,1)}, u32[]{:S(2)}, u32[]{:S(2)}) %all-to-all-start) | async-done | bytes 1048608 | tf_op jit(solution)/shard_map/all_to_all | solution.py:147
  115.1 1.4 fusion.76
  116.6 1.3 bitcast_convert_fusion
  117.9 3.0 %copy.95 = bf16[4,16,16,16,16]{4,3,2,1,0:T(8,128)(2,1)} copy(bf16[4,16,16,16,16]{4,2,3,1,0:T(8,128)(2,1)S(1)} %bitcast_convert_fusion) | data formatting | bytes 1048576 | tf_op jit(solution)/shard_map/convert_element_type | solution.py:26
  120.9 5.8 %convert_element_type.146 = bf16[4,16,16,2,128]{4,3,2,1,0:T(2,128)(2,1)S(1)} reshape(bf16[4,16,16,16,16]{4,3,2,1,0:T(8,128)(2,1)} %copy.95) | data formatting | bytes 1048576 | tf_op jit(solution)/shard_map/convert_element_type | solution.py:26
  126.7 0.9 copy.96
  127.7 3.6 %all-to-all-start.1 = ((bf16[32,4,16,128]{3,2,1,0:T(8,128)(2,1)}), bf16[32,4,16,128]{3,2,1,0:T(8,128)(2,1)S(1)}, u32[]{:S(2)}, u32[]{:S(2)}) async-start(bf16[32,4,16,128]{3,2,1,0:T(8,128)(2,1)} %bitcast.34), calls=%async_computation.1 | async-start | bytes 1048576 | tf_op jit(solution)/shard_map/all_to_all | solution.py:151
  131.6 8.5 %psum.15 = bf16[8,16]{1,0:T(8,128)(2,1)S(1)} all-reduce(bf16[8,16]{1,0:T(8,128)(2,1)S(1)} %copy.104), channel_id=1, replica_groups=mesh['groups'=1,'row'=16,'col'=2] {'col'}, use_global_device_ids=true, to_apply=%region_14.15 | all-reduce | flops 128 | bytes 512 | tf_op jit(solution)/shard_map/psum | solution.py:120
  140.2 2.1 %fusion.26 = f32[2048,128]{1,0:T(8,128)} fusion(bf16[2048,128]{1,0:T(8,128)(2,1)S(1)} %copy-done.5, bf16[128,640]{1,0:T(8,128)(2,1)} %param.26), kind=kOutput, calls=%fused_computation.39 | convolution fusion | flops 67895296 | bytes 1605632 | tf_op jit(solution)/shard_map/dot_general | solution.py:158
  142.3 3.7 %all-reduce.2.cloned.1.call-done = bf16[8,16,64,32]{2,3,1,0:T(8,128)(2,1)} async-done(((bf16[8,16,64,32]{2,3,1,0:T(8,128)(2,1)}), bf16[8,16,64,32]{2,3,1,0:T(8,128)(2,1)}) %all-reduce.2.cloned.1.call-update) | async-done | bytes 524304 | tf_op jit(solution)/shard_map/psum | solution.py:119
  146.1 2.5 %fusion.32 = bf16[64,16,64]{2,0,1:T(8,128)(2,1)S(1)} fusion(bf16[8,32,64,1]{2,1,3,0:T(8,128)(2,1)S(1)} %bitcast.239, bf16[8,16,64,32]{2,3,1,0:T(8,128)(2,1)} %all-reduce.2.cloned.1.call-done, bf16[64,8,32,1]{0,2,3,1:T(8,128)(2,1)S(1)} %bitcast.238, f32[8,16]{1,0:T(8,128)S(1)} %convert_element_type.161, f32[64,16]{0,1:T(8,128)S(1)} %add_sqrt_fusion.2, ...), kind=kOutput, calls=%fused_computation.49 | convolution fusion | flops 69533696 | bytes 860736 | tf_op jit(solution)/shard_map/hisc,hcm->sim/dot_general | solution.py:127
  149.9 1.8 %fusion.27 = bf16[2048,128]{1,0:T(8,128)(2,1)S(1)} fusion(f32[2048,128]{1,0:T(8,128)} %fusion.26, bf16[128,128]{1,0:T(8,128)(2,1)S(1)} %copy-done, f32[16,8,16,128]{3,2,1,0:T(8,128)S(1)} %bitcast_convert_fusion.1, f32[2048]{0:T(1024)S(1)} %sqrt_bitcast_fusion, f32[2048]{0:T(1024)S(1)} %get-tuple-element.106, bf16[2048,128]{1,0:T(8,128)(2,1)S(1)} %bitcast.227), kind=kOutput, calls=%fused_computation.41 | convolution fusion | flops 68943872 | bytes 3194880 | tf_op jit(solution)/shard_map/dot_general | solution.py:154
  151.8 4.2 %while.21 = (s32[]{:T(128)}, bf16[2,1024,128]{2,1,0:T(8,128)(2,1)S(1)}, bf16[2,1024,128]{2,1,0:T(8,128)(2,1)S(1)}, bf16[128,1024]{1,0:T(8,128)(2,1)S(1)}, bf16[512,128]{1,0:T(8,128)(2,1)S(1)}, /*index=5*/s32[]{:T(128)}) while((s32[]{:T(128)}, bf16[2,1024,128]{2,1,0:T(8,128)(2,1)S(1)}, bf16[2,1024,128]{2,1,0:T(8,128)(2,1)S(1)}, ...), condition=%wide.region_11.12_spmd, body=%wide.region_8.11_spmd.sunk | while | flops 407503872 | bytes 10129493 | solution.py:176
  (109 shorter events, 24.8 us)
Async XLA Ops:
  7.2 142.7 %copy-start = (bf16[128,128]{1,0:T(8,128)(2,1)S(1)}, bf16[128,128]{1,0:T(8,128)(2,1)}, u32[]{:S(2)}) copy-start(bf16[128,128]{1,0:T(8,128)(2,1)} %param.27) | copy-start | bytes 98308
  7.2 51.0 %all-gather.2.cloned.1.call-start = ((), (), s32[]{:S(2)}) async-start(), calls=%async_computation.2 | async-start | bytes 2228224 | tf_op jit(solution)/shard_map/all_gather | solution.py:61
  11.9 2.0 %copy-start.14 = (s32[256]{0:T(256)S(1)}, s32[256]{0:T(256)}, u32[]{:S(2)}) copy-start(s32[256]{0:T(256)} %param.20) | copy-start | bytes 3076
  11.9 2.2 %copy-start.9 = (bf16[64,64]{1,0:T(8,128)(2,1)S(1)}, bf16[64,64]{1,0:T(8,128)(2,1)}, u32[]{:S(2)}) copy-start(bf16[64,64]{1,0:T(8,128)(2,1)} %param.21) | copy-start | bytes 24580
  63.8 1.3 copy-start.1
  70.4 1.0 copy-start.11
  70.4 1.1 copy-start.12
  75.0 1.0 copy-start.11
  75.0 1.1 copy-start.12
  77.0 2.3 %copy-start.6 = (bf16[128,640]{1,0:T(8,128)(2,1)S(1)}, bf16[128,640]{1,0:T(8,128)(2,1)}, u32[]{:S(2)}) copy-start(bf16[128,640]{1,0:T(8,128)(2,1)} %param.26) | copy-start | bytes 491524
  78.5 0.8 copy-start.4
  84.2 5.0 %copy-start.7 = (bf16[64,512]{1,0:T(8,128)(2,1)S(1)}, bf16[64,512]{1,0:T(8,128)(2,1)}, u32[]{:S(2)}) copy-start(bf16[64,512]{1,0:T(8,128)(2,1)} %param.24) | copy-start | bytes 196612
  84.2 5.1 %copy-start.2 = (bf16[64,128,64]{2,1,0:T(8,128)(2,1)S(1)}, bf16[64,128,64]{2,1,0:T(8,128)(2,1)}, u32[]{:S(2)}) copy-start(bf16[64,128,64]{2,1,0:T(8,128)(2,1)} %copy-done.1) | copy-start | bytes 3145732
  85.5 29.6 %all-to-all-start = ((bf16[2,32,4,16,128]{4,3,2,0,1:T(8,128)(2,1)}), bf16[2,32,4,16,128]{4,3,2,0,1:T(8,128)(2,1)}, u32[]{:S(2)}, u32[]{:S(2)}) async-start(bf16[2,32,4,16,128]{4,3,2,0,1:T(8,128)(2,1)} %copy.92), calls=%async_computation | async-start | bytes 2097152 | tf_op jit(solution)/shard_map/all_to_all | solution.py:147
  88.9 57.1 %all-reduce.2.cloned.1.call-start = ((), (), s32[]{:S(2)}) async-start(), calls=%async_computation.3 | async-start | bytes 2097152 | tf_op jit(solution)/shard_map/psum | solution.py:119
  90.6 1.5 copy-start.10
  126.7 4.7 %copy-start.8 = (bf16[256,64]{0,1:T(8,128)(2,1)S(1)}, bf16[256,64]{0,1:T(8,128)(2,1)}, u32[]{:S(2)}) copy-start(bf16[256,64]{0,1:T(8,128)(2,1)} %param.25) | copy-start | bytes 98308
  126.7 13.5 %copy-start.5 = (bf16[2048,128]{1,0:T(8,128)(2,1)S(1)}, bf16[2048,128]{1,0:T(8,128)(2,1)}, u32[]{:S(2)}) copy-start(bf16[2048,128]{1,0:T(8,128)(2,1)} %copy-done.4) | copy-start | bytes 1572868
  127.7 21.7 %all-to-all-start.1 = ((bf16[32,4,16,128]{3,2,1,0:T(8,128)(2,1)}), bf16[32,4,16,128]{3,2,1,0:T(8,128)(2,1)S(1)}, u32[]{:S(2)}, u32[]{:S(2)}) async-start(bf16[32,4,16,128]{3,2,1,0:T(8,128)(2,1)} %bitcast.34), calls=%async_computation.1 | async-start | bytes 1048576 | tf_op jit(solution)/shard_map/all_to_all | solution.py:151
  149.9 1.8 %copy-start.3 = (bf16[128,1024]{1,0:T(8,128)(2,1)S(1)}, bf16[128,1024]{1,0:T(8,128)(2,1)}, u32[]{:S(2)}) copy-start(bf16[128,1024]{1,0:T(8,128)(2,1)} %param.28) | copy-start | bytes 786436
  149.9 1.8 %copy-start.13 = (bf16[512,128]{1,0:T(8,128)(2,1)S(1)}, bf16[512,128]{1,0:T(8,128)(2,1)}, u32[]{:S(2)}) copy-start(bf16[512,128]{1,0:T(8,128)(2,1)} %param.29) | copy-start | bytes 393220
  156.0 0.8 copy-start.15
Sparse Core Ops, SparseCore 0:
  14.0 44.1 all-gather.1
  97.1 48.9 all-reduce.1
where the time goes:
time: 165 us; the launch traced here: 164 us
  waiting for transfers between devices  64.8 us (39%)
  local copies, waits for them, and re-layouts  40.2 us (24%)
  matrix products  19.4 us (12%)
  between operations  14.5 us (9%)
  blocking collectives  8.55 us (5%)
  other arithmetic  8.53 us (5%)
  starting transfers between devices  7.4 us (4%)
    all_gather x1, waiting for transfers between devices, on_device(): gathered = lax.all_gather(align_rows, 'row', axis=1, tiled=True)  42.9 us
    all_to_all x1, waiting for transfers between devices, on_device(): lax.all_to_all(grouped, ('row', 'col'), split_axis=1, concat_axis=1, tile...  18.1 us
    convert_element_type x3, local copies, waits for them, and re-layouts, triangle_product(): return product.transpose(1, 3, 0, 2, 4).astype(jnp.bfloat16)  9.76 us
    psum x1, blocking collectives, on_device(): lax.psum(partial_total.astype(jnp.bfloat16), 'col').astype(jnp.float32)  8.55 us
    unnamed x36, local copies, waits for them, and re-layouts  6.61 us
    psum x1, waiting for transfers between devices, on_device(): lax.psum(partial_sum.astype(jnp.bfloat16), 'col').astype(jnp.float32)  3.71 us
    all_to_all x1, starting transfers between devices, on_device(): lax.all_to_all(flat_result, ('row', 'col'), split_axis=0, concat_axis=0,...  3.64 us
    all_to_all x1, starting transfers between devices, on_device(): lax.all_to_all(grouped, ('row', 'col'), split_axis=1, concat_axis=1, tile...  3.46 us
  transfers between devices with their start and end apart: 4, of which 3 were waited for; matrix products, arithmetic and copies ran while one was open for 17% of the time, Pallas kernels for 0%

commit v1 on v0

--- a/solution.py
+++ b/solution.py
@@ -1,9 +1,23 @@
+import functools
 import jax
 import jax.numpy as jnp
 from jax import lax
 from jax.sharding import PartitionSpec as P
 
 epsilon = 1e-05
+
+
+def time_target_by_axis(xin, net_axis):
+    world = lax.axis_size(net_axis)
+    pool = [xin]
+    for b in range(world - 1):
+        pool.append(lax.ppermute(pool[-1], net_axis, [(k, (k + 1) % world) for k in range(world)]))
+    return jnp.roll(
+        jnp.concatenate(pool[::-1], axis=1), (lax.axis_index(net_axis) + 1) * xin.shape[1], axis=1
+    )
+
+
+fields_replace = functools.partial(time_target_by_axis, net_axis="row")
 
 
 def normalize(values, channel_dim):
@@ -58,7 +72,7 @@
     alignments = jnp.take(alignment_pool, sample_index, axis=0)
     align_norm = normalize(alignments, 2).astype(jnp.bfloat16)
     align_rows = align_norm.reshape(samples, tok_row * align_width)
-    gathered = lax.all_gather(align_rows, "row", axis=1, tiled=True)
+    gathered = fields_replace(align_rows)
     column_flat = lax.dynamic_slice_in_dim(
         gathered, column_start * align_width, tok_col * align_width, 1
     )

time: 165 us -> 228 us (1.38)
  waiting for transfers between devices: 64.8 us -> 127 us
    ppermute x0 -> x15, waiting for transfers between devices: none -> 105 us  [time_target_by_axis(): lax.ppermute(pool[-1], net_axis, [(k, (k + 1) % world) for k in range(wor...]
    all_gather x1 -> x0, waiting for transfers between devices: 42.9 us -> none  [on_device(): gathered = lax.all_gather(align_rows, 'row', axis=1, tiled=True)]
    unnamed x36 -> x67, local copies, waits for them, and re-layouts: 6.61 us -> 7.92 us
  transfers between devices with their start and end apart: 4 -> 18, of which waited for: 3 -> 17; matrix products, arithmetic and copies ran while one was open for 17% -> 12% of each run, Pallas kernels for 0% -> 0%
where the time goes in v1:
time: 228 us; the launch traced here: 227 us
  waiting for transfers between devices  127 us (56%)
  local copies, waits for them, and re-layouts  40.2 us (18%)
  matrix products  19.4 us (9%)
  between operations  14.8 us (6%)
  other arithmetic  9.22 us (4%)
  blocking collectives  8.54 us (4%)
  starting transfers between devices  7.78 us (3%)
    ppermute x15, waiting for transfers between devices, time_target_by_axis(): lax.ppermute(pool[-1], net_axis, [(k, (k + 1) % world) for k in range(wor...  105 us
    all_to_all x1, waiting for transfers between devices, on_device(): lax.all_to_all(grouped, ('row', 'col'), split_axis=1, concat_axis=1, tile...  18.1 us
    convert_element_type x3, local copies, waits for them, and re-layouts, triangle_product(): return product.transpose(1, 3, 0, 2, 4).astype(jnp.bfloat16)  9.85 us
    psum x1, blocking collectives, on_device(): lax.psum(partial_total.astype(jnp.bfloat16), 'col').astype(jnp.float32)  8.54 us
    unnamed x67, local copies, waits for them, and re-layouts  7.92 us
  transfers between devices with their start and end apart: 18, of which 17 were waited for; matrix products, arithmetic and copies ran while one was open for 12% of the time, Pallas kernels for 0%

profile of v1, /device:TPU:0, one launch (start us, length us, event | category | flops | bytes accessed | tf_op | source)
XLA Modules:
  0.0 227.4 jit_solution(2968636050808624985)
XLA Ops:
  8.5 2.0 copy.82
  13.7 7.6 %collective-permute-done = bf16[64,1024]{1,0:T(8,128)(2,1)S(1)} collective-permute-done((bf16[64,1024]{1,0:T(8,128)(2,1)S(1)}, bf16[64,1024]{1,0:T(8,128)(2,1)S(1)}, u32[]{:S(2)}, u32[]{:S(2)}) %collective-permute-start) | collective-permute-done | bytes 131104 | tf_op jit(solution)/shard_map/ppermute | solution.py:14
  21.3 7.1 %collective-permute-done.1 = bf16[64,1024]{1,0:T(8,128)(2,1)S(1)} collective-permute-done((bf16[64,1024]{1,0:T(8,128)(2,1)S(1)}, bf16[64,1024]{1,0:T(8,128)(2,1)S(1)}, u32[]{:S(2)}, u32[]{:S(2)}) %collective-permute-start.1) | collective-permute-done | bytes 131104 | tf_op jit(solution)/shard_map/ppermute | solution.py:14
  28.4 7.1 %collective-permute-done.2 = bf16[64,1024]{1,0:T(8,128)(2,1)S(1)} collective-permute-done((bf16[64,1024]{1,0:T(8,128)(2,1)S(1)}, bf16[64,1024]{1,0:T(8,128)(2,1)S(1)}, u32[]{:S(2)}, u32[]{:S(2)}) %collective-permute-start.2) | collective-permute-done | bytes 131104 | tf_op jit(solution)/shard_map/ppermute | solution.py:14
  35.5 7.1 %collective-permute-done.3 = bf16[64,1024]{1,0:T(8,128)(2,1)S(1)} collective-permute-done((bf16[64,1024]{1,0:T(8,128)(2,1)S(1)}, bf16[64,1024]{1,0:T(8,128)(2,1)S(1)}, u32[]{:S(2)}, u32[]{:S(2)}) %collective-permute-start.3) | collective-permute-done | bytes 131104 | tf_op jit(solution)/shard_map/ppermute | solution.py:14
  42.6 7.1 %collective-permute-done.4 = bf16[64,1024]{1,0:T(8,128)(2,1)S(1)} collective-permute-done((bf16[64,1024]{1,0:T(8,128)(2,1)S(1)}, bf16[64,1024]{1,0:T(8,128)(2,1)S(1)}, u32[]{:S(2)}, u32[]{:S(2)}) %collective-permute-start.4) | collective-permute-done | bytes 131104 | tf_op jit(solution)/shard_map/ppermute | solution.py:14
  49.7 7.1 %collective-permute-done.5 = bf16[64,1024]{1,0:T(8,128)(2,1)S(1)} collective-permute-done((bf16[64,1024]{1,0:T(8,128)(2,1)S(1)}, bf16[64,1024]{1,0:T(8,128)(2,1)S(1)}, u32[]{:S(2)}, u32[]{:S(2)}) %collective-permute-start.5) | collective-permute-done | bytes 131104 | tf_op jit(solution)/shard_map/ppermute | solution.py:14
  56.8 7.1 %collective-permute-done.6 = bf16[64,1024]{1,0:T(8,128)(2,1)S(1)} collective-permute-done((bf16[64,1024]{1,0:T(8,128)(2,1)S(1)}, bf16[64,1024]{1,0:T(8,128)(2,1)S(1)}, u32[]{:S(2)}, u32[]{:S(2)}) %collective-permute-start.6) | collective-permute-done | bytes 131104 | tf_op jit(solution)/shard_map/ppermute | solution.py:14
  63.9 7.1 %collective-permute-done.7 = bf16[64,1024]{1,0:T(8,128)(2,1)S(1)} collective-permute-done((bf16[64,1024]{1,0:T(8,128)(2,1)S(1)}, bf16[64,1024]{1,0:T(8,128)(2,1)S(1)}, u32[]{:S(2)}, u32[]{:S(2)}) %collective-permute-start.7) | collective-permute-done | bytes 131104 | tf_op jit(solution)/shard_map/ppermute | solution.py:14
  71.0 7.1 %collective-permute-done.8 = bf16[64,1024]{1,0:T(8,128)(2,1)S(1)} collective-permute-done((bf16[64,1024]{1,0:T(8,128)(2,1)S(1)}, bf16[64,1024]{1,0:T(8,128)(2,1)S(1)}, u32[]{:S(2)}, u32[]{:S(2)}) %collective-permute-start.8) | collective-permute-done | bytes 131104 | tf_op jit(solution)/shard_map/ppermute | solution.py:14
  78.1 7.1 %collective-permute-done.9 = bf16[64,1024]{1,0:T(8,128)(2,1)S(1)} collective-permute-done((bf16[64,1024]{1,0:T(8,128)(2,1)S(1)}, bf16[64,1024]{1,0:T(8,128)(2,1)S(1)}, u32[]{:S(2)}, u32[]{:S(2)}) %collective-permute-start.9) | collective-permute-done | bytes 131104 | tf_op jit(solution)/shard_map/ppermute | solution.py:14
  85.1 7.1 %collective-permute-done.10 = bf16[64,1024]{1,0:T(8,128)(2,1)S(1)} collective-permute-done((bf16[64,1024]{1,0:T(8,128)(2,1)S(1)}, bf16[64,1024]{1,0:T(8,128)(2,1)S(1)}, u32[]{:S(2)}, u32[]{:S(2)}) %collective-permute-start.10) | collective-permute-done | bytes 131104 | tf_op jit(solution)/shard_map/ppermute | solution.py:14
  92.2 7.1 %collective-permute-done.11 = bf16[64,1024]{1,0:T(8,128)(2,1)S(1)} collective-permute-done((bf16[64,1024]{1,0:T(8,128)(2,1)S(1)}, bf16[64,1024]{1,0:T(8,128)(2,1)S(1)}, u32[]{:S(2)}, u32[]{:S(2)}) %collective-permute-start.11) | collective-permute-done | bytes 131104 | tf_op jit(solution)/shard_map/ppermute | solution.py:14
  100.5 5.9 %collective-permute-done.12 = bf16[64,1024]{1,0:T(8,128)(2,1)S(1)} collective-permute-done((bf16[64,1024]{1,0:T(8,128)(2,1)S(1)}, bf16[64,1024]{1,0:T(8,128)(2,1)S(1)}, u32[]{:S(2)}, u32[]{:S(2)}) %collective-permute-start.12) | collective-permute-done | bytes 131104 | tf_op jit(solution)/shard_map/ppermute | solution.py:14
  106.6 6.9 %collective-permute-done.13 = bf16[64,1024]{1,0:T(8,128)(2,1)S(1)} collective-permute-done((bf16[64,1024]{1,0:T(8,128)(2,1)S(1)}, bf16[64,1024]{1,0:T(8,128)(2,1)S(1)}, u32[]{:S(2)}, u32[]{:S(2)}) %collective-permute-start.13) | collective-permute-done | bytes 131104 | tf_op jit(solution)/shard_map/ppermute | solution.py:14
  113.6 7.0 %collective-permute-done.14 = bf16[64,1024]{1,0:T(8,128)(2,1)S(1)} collective-permute-done((bf16[64,1024]{1,0:T(8,128)(2,1)S(1)}, bf16[64,1024]{1,0:T(8,128)(2,1)S(1)}, u32[]{:S(2)}, u32[]{:S(2)}) %collective-permute-start.14) | collective-permute-done | bytes 131104 | tf_op jit(solution)/shard_map/ppermute | solution.py:14
  122.5 3.3 %reshape.294 = bf16[64,128,64]{2,1,0:T(8,128)(2,1)S(1)} reshape(bf16[64,8192]{1,0:T(8,128)(2,1)} %constant_dynamic-slice_fusion.1) | data formatting | bytes 2097152 | tf_op jit(solution)/shard_map/reshape | solution.py:79
  128.0 1.7 copy.89
  129.8 8.8 %while.20 = (s32[]{:T(128)}, bf16[2,8,128,128]{3,2,1,0:T(8,128)(2,1)S(1)}, bf16[2,8,128,128]{3,2,1,0:T(8,128)(2,1)}, bf16[2,64,256]{1,2,0:T(8,128)(2,1)}, bf16[6...) while((s32[]{:T(128)}, bf16[2,8,128,128]{3,2,1,0:T(8,128)(2,1)S(1)}, ...), condition=%wide.region_3.4_spmd, body=%wide.region_2.3_spmd.sunk | while | flops 405143552 | bytes 13992077 | solution.py:112
  149.4 3.4 %all-to-all-start = ((bf16[2,32,4,16,128]{4,3,2,0,1:T(8,128)(2,1)}), bf16[2,32,4,16,128]{4,3,2,0,1:T(8,128)(2,1)}, u32[]{:S(2)}, u32[]{:S(2)}) async-start(bf16[2,32,4,16,128]{4,3,2,0,1:T(8,128)(2,1)} %copy.92), calls=%async_computation | async-start | bytes 2097152 | tf_op jit(solution)/shard_map/all_to_all | solution.py:161
  157.5 1.6 reshape.302
  159.1 1.6 copy.103
  160.8 18.1 %all-to-all-done = bf16[2,32,4,16,128]{4,3,2,0,1:T(8,128)(2,1)} async-done(((bf16[2,32,4,16,128]{4,3,2,0,1:T(8,128)(2,1)}), bf16[2,32,4,16,128]{4,3,2,0,1:T(8,128)(2,1)}, u32[]{:S(2)}, u32[]{:S(2)}) %all-to-all-start) | async-done | bytes 1048608 | tf_op jit(solution)/shard_map/all_to_all | solution.py:161
  181.7 3.0 %copy.95 = bf16[4,16,16,16,16]{4,3,2,1,0:T(8,128)(2,1)} copy(bf16[4,16,16,16,16]{4,2,3,1,0:T(8,128)(2,1)S(1)} %bitcast_convert_fusion) | data formatting | bytes 1048576 | tf_op jit(solution)/shard_map/convert_element_type | solution.py:40
  184.7 5.9 %convert_element_type.146 = bf16[4,16,16,2,128]{4,3,2,1,0:T(2,128)(2,1)S(1)} reshape(bf16[4,16,16,16,16]{4,3,2,1,0:T(8,128)(2,1)} %copy.95) | data formatting | bytes 1048576 | tf_op jit(solution)/shard_map/convert_element_type | solution.py:40
  191.5 3.6 %all-to-all-start.1 = ((bf16[32,4,16,128]{3,2,1,0:T(8,128)(2,1)}), bf16[32,4,16,128]{3,2,1,0:T(8,128)(2,1)S(1)}, u32[]{:S(2)}, u32[]{:S(2)}) async-start(bf16[32,4,16,128]{3,2,1,0:T(8,128)(2,1)} %bitcast.34), calls=%async_computation.1 | async-start | bytes 1048576 | tf_op jit(solution)/shard_map/all_to_all | solution.py:165
  195.4 8.5 %psum.15 = bf16[8,16]{1,0:T(8,128)(2,1)S(1)} all-reduce(bf16[8,16]{1,0:T(8,128)(2,1)S(1)} %copy.104), channel_id=1, replica_groups=mesh['groups'=1,'row'=16,'col'=2] {'col'}, use_global_device_ids=true, to_apply=%region_14.15 | all-reduce | flops 128 | bytes 512 | tf_op jit(solution)/shard_map/psum | solution.py:134
  204.0 2.2 fusion.26
  206.1 3.7 %all-reduce.2.cloned.1.call-done = bf16[8,16,64,32]{2,3,1,0:T(8,128)(2,1)} async-done(((bf16[8,16,64,32]{2,3,1,0:T(8,128)(2,1)}), bf16[8,16,64,32]{2,3,1,0:T(8,128)(2,1)}) %all-reduce.2.cloned.1.call-update) | async-done | bytes 524304 | tf_op jit(solution)/shard_map/psum | solution.py:133
  209.8 2.5 %fusion.32 = bf16[64,16,64]{2,0,1:T(8,128)(2,1)S(1)} fusion(bf16[8,32,64,1]{2,1,3,0:T(8,128)(2,1)S(1)} %bitcast.239, bf16[8,16,64,32]{2,3,1,0:T(8,128)(2,1)} %all-reduce.2.cloned.1.call-done, bf16[64,8,32,1]{0,2,3,1:T(8,128)(2,1)S(1)} %bitcast.238, f32[8,16]{1,0:T(8,128)S(1)} %convert_element_type.161, f32[64,16]{0,1:T(8,128)S(1)} %add_sqrt_fusion.2, ...), kind=kOutput, calls=%fused_computation.49 | convolution fusion | flops 69533696 | bytes 860736 | tf_op jit(solution)/shard_map/hisc,hcm->sim/dot_general | solution.py:141
  213.7 1.8 fusion.27
  215.5 4.2 %while.21 = (s32[]{:T(128)}, bf16[2,1024,128]{2,1,0:T(8,128)(2,1)S(1)}, bf16[2,1024,128]{2,1,0:T(8,128)(2,1)S(1)}, bf16[128,1024]{1,0:T(8,128)(2,1)S(1)}, bf16[512,128]{1,0:T(8,128)(2,1)S(1)}, /*index=5*/s32[]{:T(128)}) while((s32[]{:T(128)}, bf16[2,1024,128]{2,1,0:T(8,128)(2,1)S(1)}, bf16[2,1024,128]{2,1,0:T(8,128)(2,1)S(1)}, ...), condition=%wide.region_11.12_spmd, body=%wide.region_8.11_spmd.sunk | while | flops 407503872 | bytes 10129493 | solution.py:190
  (168 shorter events, 44.2 us)
Async XLA Ops:
  7.2 206.5 %copy-start = (bf16[128,128]{1,0:T(8,128)(2,1)S(1)}, bf16[128,128]{1,0:T(8,128)(2,1)}, u32[]{:S(2)}) copy-start(bf16[128,128]{1,0:T(8,128)(2,1)} %param.27) | copy-start | bytes 98308
  7.2 92.1 %copy-start.9 = (bf16[64,64]{1,0:T(8,128)(2,1)S(1)}, bf16[64,64]{1,0:T(8,128)(2,1)}, u32[]{:S(2)}) copy-start(bf16[64,64]{1,0:T(8,128)(2,1)} %param.21) | copy-start | bytes 24580
  8.5 97.9 %copy-start.14 = (s32[256]{0:T(256)S(1)}, s32[256]{0:T(256)}, u32[]{:S(2)}) copy-start(s32[256]{0:T(256)} %param.20) | copy-start | bytes 3076
  13.1 8.2 %collective-permute-start = (bf16[64,1024]{1,0:T(8,128)(2,1)S(1)}, bf16[64,1024]{1,0:T(8,128)(2,1)S(1)}, u32[]{:S(2)}, u32[]{:S(2)}) collective-permute-start(bf16[64,1024]{1,0:T(8,128)(2,1)S(1)} %divide_convert_fusion), channel_id=1, source_target_pairs={{0,2},{2,4},{4,6},{6,8},{8,10},{10,12},{12,14},{14,16},{16,18},{18... | collective-permute-start | bytes 393224 | tf_op jit(solution)/shard_map/ppermute | solution.py:14
  21.3 7.1 %collective-permute-start.1 = (bf16[64,1024]{1,0:T(8,128)(2,1)S(1)}, bf16[64,1024]{1,0:T(8,128)(2,1)S(1)}, u32[]{:S(2)}, u32[]{:S(2)}) collective-permute-start(bf16[64,1024]{1,0:T(8,128)(2,1)S(1)} %collective-permute-done), channel_id=1, source_target_pairs={{0,2},{2,4},{4,6},{6,8},{8,10},{10,12},{12,14},{14,16},{16,18},{18... | collective-permute-start | bytes 393224 | tf_op jit(solution)/shard_map/ppermute | solution.py:14
  28.4 7.1 %collective-permute-start.2 = (bf16[64,1024]{1,0:T(8,128)(2,1)S(1)}, bf16[64,1024]{1,0:T(8,128)(2,1)S(1)}, u32[]{:S(2)}, u32[]{:S(2)}) collective-permute-start(bf16[64,1024]{1,0:T(8,128)(2,1)S(1)} %collective-permute-done.1), channel_id=1, source_target_pairs={{0,2},{2,4},{4,6},{6,8},{8,10},{10,12},{12,14},{14,16},{16,18},{18... | collective-permute-start | bytes 393224 | tf_op jit(solution)/shard_map/ppermute | solution.py:14
  35.5 7.1 %collective-permute-start.3 = (bf16[64,1024]{1,0:T(8,128)(2,1)S(1)}, bf16[64,1024]{1,0:T(8,128)(2,1)S(1)}, u32[]{:S(2)}, u32[]{:S(2)}) collective-permute-start(bf16[64,1024]{1,0:T(8,128)(2,1)S(1)} %collective-permute-done.2), channel_id=1, source_target_pairs={{0,2},{2,4},{4,6},{6,8},{8,10},{10,12},{12,14},{14,16},{16,18},{18... | collective-permute-start | bytes 393224 | tf_op jit(solution)/shard_map/ppermute | solution.py:14
  42.6 7.1 %collective-permute-start.4 = (bf16[64,1024]{1,0:T(8,128)(2,1)S(1)}, bf16[64,1024]{1,0:T(8,128)(2,1)S(1)}, u32[]{:S(2)}, u32[]{:S(2)}) collective-permute-start(bf16[64,1024]{1,0:T(8,128)(2,1)S(1)} %collective-permute-done.3), channel_id=1, source_target_pairs={{0,2},{2,4},{4,6},{6,8},{8,10},{10,12},{12,14},{14,16},{16,18},{18... | collective-permute-start | bytes 393224 | tf_op jit(solution)/shard_map/ppermute | solution.py:14
  49.7 7.1 %collective-permute-start.5 = (bf16[64,1024]{1,0:T(8,128)(2,1)S(1)}, bf16[64,1024]{1,0:T(8,128)(2,1)S(1)}, u32[]{:S(2)}, u32[]{:S(2)}) collective-permute-start(bf16[64,1024]{1,0:T(8,128)(2,1)S(1)} %collective-permute-done.4), channel_id=1, source_target_pairs={{0,2},{2,4},{4,6},{6,8},{8,10},{10,12},{12,14},{14,16},{16,18},{18... | collective-permute-start | bytes 393224 | tf_op jit(solution)/shard_map/ppermute | solution.py:14
  56.8 7.1 %collective-permute-start.6 = (bf16[64,1024]{1,0:T(8,128)(2,1)S(1)}, bf16[64,1024]{1,0:T(8,128)(2,1)S(1)}, u32[]{:S(2)}, u32[]{:S(2)}) collective-permute-start(bf16[64,1024]{1,0:T(8,128)(2,1)S(1)} %collective-permute-done.5), channel_id=1, source_target_pairs={{0,2},{2,4},{4,6},{6,8},{8,10},{10,12},{12,14},{14,16},{16,18},{18... | collective-permute-start | bytes 393224 | tf_op jit(solution)/shard_map/ppermute | solution.py:14
  63.9 7.1 %collective-permute-start.7 = (bf16[64,1024]{1,0:T(8,128)(2,1)S(1)}, bf16[64,1024]{1,0:T(8,128)(2,1)S(1)}, u32[]{:S(2)}, u32[]{:S(2)}) collective-permute-start(bf16[64,1024]{1,0:T(8,128)(2,1)S(1)} %collective-permute-done.6), channel_id=1, source_target_pairs={{0,2},{2,4},{4,6},{6,8},{8,10},{10,12},{12,14},{14,16},{16,18},{18... | collective-permute-start | bytes 393224 | tf_op jit(solution)/shard_map/ppermute | solution.py:14
  71.0 7.1 %collective-permute-start.8 = (bf16[64,1024]{1,0:T(8,128)(2,1)S(1)}, bf16[64,1024]{1,0:T(8,128)(2,1)S(1)}, u32[]{:S(2)}, u32[]{:S(2)}) collective-permute-start(bf16[64,1024]{1,0:T(8,128)(2,1)S(1)} %collective-permute-done.7), channel_id=1, source_target_pairs={{0,2},{2,4},{4,6},{6,8},{8,10},{10,12},{12,14},{14,16},{16,18},{18... | collective-permute-start | bytes 393224 | tf_op jit(solution)/shard_map/ppermute | solution.py:14
  78.1 7.1 %collective-permute-start.9 = (bf16[64,1024]{1,0:T(8,128)(2,1)S(1)}, bf16[64,1024]{1,0:T(8,128)(2,1)S(1)}, u32[]{:S(2)}, u32[]{:S(2)}) collective-permute-start(bf16[64,1024]{1,0:T(8,128)(2,1)S(1)} %collective-permute-done.8), channel_id=1, source_target_pairs={{0,2},{2,4},{4,6},{6,8},{8,10},{10,12},{12,14},{14,16},{16,18},{18... | collective-permute-start | bytes 393224 | tf_op jit(solution)/shard_map/ppermute | solution.py:14
  85.1 7.1 %collective-permute-start.10 = (bf16[64,1024]{1,0:T(8,128)(2,1)S(1)}, bf16[64,1024]{1,0:T(8,128)(2,1)S(1)}, u32[]{:S(2)}, u32[]{:S(2)}) collective-permute-start(bf16[64,1024]{1,0:T(8,128)(2,1)S(1)} %collective-permute-done.9), channel_id=1, source_target_pairs={{0,2},{2,4},{4,6},{6,8},{8,10},{10,12},{12,14},{14,16},{16,18},{18... | collective-permute-start | bytes 393224 | tf_op jit(solution)/shard_map/ppermute | solution.py:14
  92.2 7.1 %collective-permute-start.11 = (bf16[64,1024]{1,0:T(8,128)(2,1)S(1)}, bf16[64,1024]{1,0:T(8,128)(2,1)S(1)}, u32[]{:S(2)}, u32[]{:S(2)}) collective-permute-start(bf16[64,1024]{1,0:T(8,128)(2,1)S(1)} %collective-permute-done.10), channel_id=1, source_target_pairs={{0,2},{2,4},{4,6},{6,8},{8,10},{10,12},{12,14},{14,16},{16,18},{18... | collective-permute-start | bytes 393224 | tf_op jit(solution)/shard_map/ppermute | solution.py:14
  99.3 7.1 %collective-permute-start.12 = (bf16[64,1024]{1,0:T(8,128)(2,1)S(1)}, bf16[64,1024]{1,0:T(8,128)(2,1)S(1)}, u32[]{:S(2)}, u32[]{:S(2)}) collective-permute-start(bf16[64,1024]{1,0:T(8,128)(2,1)S(1)} %collective-permute-done.11), channel_id=1, source_target_pairs={{0,2},{2,4},{4,6},{6,8},{8,10},{10,12},{12,14},{14,16},{16,18},{18... | collective-permute-start | bytes 393224 | tf_op jit(solution)/shard_map/ppermute | solution.py:14
  106.4 7.1 %collective-permute-start.13 = (bf16[64,1024]{1,0:T(8,128)(2,1)S(1)}, bf16[64,1024]{1,0:T(8,128)(2,1)S(1)}, u32[]{:S(2)}, u32[]{:S(2)}) collective-permute-start(bf16[64,1024]{1,0:T(8,128)(2,1)S(1)} %collective-permute-done.12), channel_id=1, source_target_pairs={{0,2},{2,4},{4,6},{6,8},{8,10},{10,12},{12,14},{14,16},{16,18},{18... | collective-permute-start | bytes 393224 | tf_op jit(solution)/shard_map/ppermute | solution.py:14
  113.5 7.1 %collective-permute-start.14 = (bf16[64,1024]{1,0:T(8,128)(2,1)S(1)}, bf16[64,1024]{1,0:T(8,128)(2,1)S(1)}, u32[]{:S(2)}, u32[]{:S(2)}) collective-permute-start(bf16[64,1024]{1,0:T(8,128)(2,1)S(1)} %collective-permute-done.13), channel_id=1, source_target_pairs={{0,2},{2,4},{4,6},{6,8},{8,10},{10,12},{12,14},{14,16},{16,18},{18... | collective-permute-start | bytes 393224 | tf_op jit(solution)/shard_map/ppermute | solution.py:14
  129.7 11.1 %copy-start.6 = (bf16[128,640]{1,0:T(8,128)(2,1)S(1)}, bf16[128,640]{1,0:T(8,128)(2,1)}, u32[]{:S(2)}) copy-start(bf16[128,640]{1,0:T(8,128)(2,1)} %param.26) | copy-start | bytes 491524
  130.7 2.6 %copy-start.11 = (bf16[2,8,128,128]{3,2,1,0:T(8,128)(2,1)S(1)}, bf16[2,8,128,128]{3,2,1,0:T(8,128)(2,1)}, u32[]{:S(2)}) copy-start(bf16[2,8,128,128]{3,2,1,0:T(8,128)(2,1)} %get-tuple-element.195) | copy-start | bytes 1572868 | tf_op jit(solution)/shard_map/while
  130.7 2.6 %copy-start.12 = (bf16[1024,128]{1,0:T(8,128)(2,1)S(1)}, bf16[1024,128]{1,0:T(8,128)(2,1)}, u32[]{:S(2)}) copy-start(bf16[1024,128]{1,0:T(8,128)(2,1)} %get-tuple-element.198) | copy-start | bytes 786436 | tf_op jit(solution)/shard_map/while
  135.0 2.6 %copy-start.11 = (bf16[2,8,128,128]{3,2,1,0:T(8,128)(2,1)S(1)}, bf16[2,8,128,128]{3,2,1,0:T(8,128)(2,1)}, u32[]{:S(2)}) copy-start(bf16[2,8,128,128]{3,2,1,0:T(8,128)(2,1)} %get-tuple-element.195) | copy-start | bytes 1572868 | tf_op jit(solution)/shard_map/while
  135.0 2.6 %copy-start.12 = (bf16[1024,128]{1,0:T(8,128)(2,1)S(1)}, bf16[1024,128]{1,0:T(8,128)(2,1)}, u32[]{:S(2)}) copy-start(bf16[1024,128]{1,0:T(8,128)(2,1)} %get-tuple-element.198) | copy-start | bytes 786436 | tf_op jit(solution)/shard_map/while
  146.3 6.7 %copy-start.7 = (bf16[64,512]{1,0:T(8,128)(2,1)S(1)}, bf16[64,512]{1,0:T(8,128)(2,1)}, u32[]{:S(2)}) copy-start(bf16[64,512]{1,0:T(8,128)(2,1)} %param.24) | copy-start | bytes 196612
  146.3 6.8 %copy-start.2 = (bf16[64,128,64]{2,1,0:T(8,128)(2,1)S(1)}, bf16[64,128,64]{2,1,0:T(8,128)(2,1)}, u32[]{:S(2)}) copy-start(bf16[64,128,64]{2,1,0:T(8,128)(2,1)} %copy-done.1) | copy-start | bytes 3145732
  149.4 29.6 %all-to-all-start = ((bf16[2,32,4,16,128]{4,3,2,0,1:T(8,128)(2,1)}), bf16[2,32,4,16,128]{4,3,2,0,1:T(8,128)(2,1)}, u32[]{:S(2)}, u32[]{:S(2)}) async-start(bf16[2,32,4,16,128]{4,3,2,0,1:T(8,128)(2,1)} %copy.92), calls=%async_computation | async-start | bytes 2097152 | tf_op jit(solution)/shard_map/all_to_all | solution.py:161
  152.7 57.1 %all-reduce.2.cloned.1.call-start = ((), (), s32[]{:S(2)}) async-start(), calls=%async_computation.2 | async-start | bytes 2097152 | tf_op jit(solution)/shard_map/psum | solution.py:133
  184.7 10.5 %copy-start.8 = (bf16[256,64]{0,1:T(8,128)(2,1)S(1)}, bf16[256,64]{0,1:T(8,128)(2,1)}, u32[]{:S(2)}) copy-start(bf16[256,64]{0,1:T(8,128)(2,1)} %param.25) | copy-start | bytes 98308
  184.7 19.3 %copy-start.5 = (bf16[2048,128]{1,0:T(8,128)(2,1)S(1)}, bf16[2048,128]{1,0:T(8,128)(2,1)}, u32[]{:S(2)}) copy-start(bf16[2048,128]{1,0:T(8,128)(2,1)} %copy-done.4) | copy-start | bytes 1572868
  191.5 21.7 %all-to-all-start.1 = ((bf16[32,4,16,128]{3,2,1,0:T(8,128)(2,1)}), bf16[32,4,16,128]{3,2,1,0:T(8,128)(2,1)S(1)}, u32[]{:S(2)}, u32[]{:S(2)}) async-start(bf16[32,4,16,128]{3,2,1,0:T(8,128)(2,1)} %bitcast.34), calls=%async_computation.1 | async-start | bytes 1048576 | tf_op jit(solution)/shard_map/all_to_all | solution.py:165
  212.3 3.2 %copy-start.3 = (bf16[128,1024]{1,0:T(8,128)(2,1)S(1)}, bf16[128,1024]{1,0:T(8,128)(2,1)}, u32[]{:S(2)}) copy-start(bf16[128,1024]{1,0:T(8,128)(2,1)} %param.28) | copy-start | bytes 786436
  212.3 3.2 %copy-start.13 = (bf16[512,128]{1,0:T(8,128)(2,1)S(1)}, bf16[512,128]{1,0:T(8,128)(2,1)}, u32[]{:S(2)}) copy-start(bf16[512,128]{1,0:T(8,128)(2,1)} %param.29) | copy-start | bytes 393220
  (4 other events, 4.4 us)
Sparse Core Ops, SparseCore 0:
  160.9 48.8 all-reduce.1
